TPU v7x, 512 devices: a whole 4x8x8 slice. The times are simulated.
512 devices in a mesh: gx: 32 (over z, x), gy: 16 (over y, core).
Axes of the slice: x: 4, y: 8, z: 8, core: 2. Of those that a mesh axis runs over, the one named last changes fastest.
Arguments:
- a_blocks: bfloat16 [32, 128, 64, 448], P('gx', 'gy'), may hold values from -0.25 to 0.25
- a_cols: int32 [32, 128, 7], P('gx', 'gy'), may hold values from 0 to 15
- mushy: int32 [32, 128], P('gx', 'gy'), may hold values 0 or 1
- p_blocks: bfloat16 [32, 128, 64, 256], P('gx', 'gy'), may hold values from -0.375 to 0.375
- p_cols: int32 [32, 128, 4], P('gx', 'gy'), may hold values from 0 to 7
- send_rows: int32 [32, 128], P('gx', 'gy'), may hold values from 0 to 7
Outputs:
- coarse_tiles: float32 [32, 512, 1536], P('gx', 'gy')
All inputs are finite; a program needn't handle non-finite values. No bound on the sum of `mushy` on one device may be relied on, other than what follows from the above.
Results may differ from a plain program's by a relative error of at most 0.0038.
Values may be sent and summed in bfloat16 or wider, within the bound.
A program may use at most 64 MiB of HBM per device.

v0:
```python
import jax
import jax.numpy as jnp
from jax import lax
from jax.sharding import PartitionSpec as P

KA = 7
KS = 3
NCOL = 8


def shifted(value, axis, by):
    length = lax.axis_size(axis)
    pairs = [(i, i + by) for i in range(length) if 0 <= i + by < length]
    return lax.ppermute(value, axis, pairs)


def dense_rows(blocks, cols, offset, width_blocks):
    count = blocks.shape[0]
    size = blocks.shape[1]
    slots = cols.shape[1]
    onehot = (
        cols[:, :, None] + offset == jnp.arange(width_blocks, dtype=jnp.int32)[None, None, :]
    ).astype(jnp.bfloat16)
    parts = blocks.reshape(count, size, slots, size)
    dense = jnp.einsum("rkc,rbka->rbca", onehot, parts, preferred_element_type=jnp.float32)
    return dense.astype(jnp.bfloat16).reshape(count, size, width_blocks * size)


def body(a_blocks, a_cols, mushy, p_blocks, p_cols, send_rows):
    ablk = a_blocks[0]
    acol = a_cols[0]
    mush = mushy[0]
    pblk = p_blocks[0]
    pcol = p_cols[0]
    sends = send_rows[0]
    rows = pblk.shape[0]
    size = pblk.shape[1]
    half = sends.shape[0] // 2
    from_left = shifted((pblk, pcol, sends), "gx", 1)
    from_right = shifted((pblk, pcol, sends), "gx", -1)
    left_sel = from_left[2][half:]
    right_sel = from_right[2][:half]
    left_blk = from_left[0][left_sel]
    left_col = from_left[1][left_sel]
    right_blk = from_right[0][right_sel]
    right_col = from_right[1][right_sel]
    extended = jnp.concatenate(
        [
            dense_rows(pblk, pcol, NCOL, 3 * NCOL),
            dense_rows(left_blk, left_col, 0, 3 * NCOL),
            dense_rows(right_blk, right_col, 2 * NCOL, 3 * NCOL),
        ],
        axis=0,
    )
    limit = jnp.where(mush > 0, KA, KS).astype(jnp.int32)
    total = jnp.zeros((rows, size, 3 * NCOL * size), jnp.float32)
    for slot in range(KA):
        live = (slot < limit).astype(jnp.bfloat16)
        ablock = ablk[:, :, slot * size : (slot + 1) * size] * live[:, None, None]
        picked = extended[acol[:, slot]]
        total = total + jnp.einsum(
            "nij,njw->niw", ablock, picked, preferred_element_type=jnp.float32
        )
    product = total.astype(jnp.bfloat16)
    own = dense_rows(pblk, pcol, 0, NCOL)
    share = NCOL * size // lax.axis_size("gy")
    summed = lax.psum(
        jnp.einsum("nbc,nbw->cw", own, product, preferred_element_type=jnp.float32), "gy"
    )
    result = lax.dynamic_slice_in_dim(summed, lax.axis_index("gy") * share, share, 0)
    return result[None]


def solution(mesh):
    placed = (
        P("gx", "gy", None, None),
        P("gx", "gy", None),
        P("gx", "gy"),
        P("gx", "gy", None, None),
        P("gx", "gy", None),
        P("gx", "gy"),
    )
    return jax.shard_map(
        body, mesh=mesh, in_specs=placed, out_specs=P("gx", "gy", None), check_vma=False
    )
```

profile of v0, /device:TPU:1, one launch (start us, length us, event | category | flops | bytes accessed | tf_op | source)
XLA Modules:
  0.0 230.6 jit_solution(7626331913532832437)
XLA Ops:
  6.5 4.6 %collective-permute-start = (bf16[8,64,256]{2,1,0:T(8,128)(2,1)}, bf16[8,64,256]{2,1,0:T(8,128)(2,1)}, u32[]{:S(2)}, u32[]{:S(2)}) collective-permute-start(bf16[8,64,256]{2,1,0:T(8,128)(2,1)} %bitcast.81), channel_id=1, source_target_pairs={{0,16},{16,32},{32,48},{48,64},{64,80},{80,96},{96,112},{112,128},... | collective-permute-start | bytes 786440 | tf_op jit(solution)/shard_map/ppermute | solution.py:14
  11.2 1.3 collective-permute-start.3
  12.5 4.0 %collective-permute-start.1 = (s32[8]{0:T(128)}, s32[8]{0:T(128)S(1)}, u32[]{:S(2)}, u32[]{:S(2)}) collective-permute-start(s32[8]{0:T(128)} %bitcast.85), channel_id=1, source_target_pairs={{0,16},{16,32},{32,48},{48,64},{64,80},{80,96},{96,112},{112,128},... | collective-permute-start | bytes 104 | tf_op jit(solution)/shard_map/ppermute | solution.py:14
  16.5 1.3 collective-permute-start.4
  18.5 4.0 %collective-permute-start.2 = (s32[8,4]{1,0:T(8,128)S(1)}, s32[8,4]{1,0:T(8,128)S(1)}, u32[]{:S(2)}, u32[]{:S(2)}) collective-permute-start(s32[8,4]{1,0:T(8,128)S(1)} %copy.12), channel_id=1, source_target_pairs={{0,16},{16,32},{32,48},{48,64},{64,80},{80,96},{96,112},{112,128},... | collective-permute-start | bytes 392 | tf_op jit(solution)/shard_map/ppermute | solution.py:14
  22.5 1.2 reshape_squeeze.4
  25.1 1.4 reshape.102
  26.6 2.7 %convert_bitcast_fusion = bf16[8,64,24,64]{3,2,1,0:T(8,128)(2,1)S(1)} fusion(bf16[8,64,4,64]{3,2,1,0:T(4,128)(2,1)} %copy-done.5, s32[8,4]{1,0:T(8,128)S(1)} %copy.13), kind=kOutput, calls=%fused_computation.18 | convolution fusion | flops 7078656 | bytes 1835136 | tf_op jit(solution)/shard_map/rkc,rbka->rbca/dot_general | solution.py:25
  29.3 3.0 %reshape.103 = bf16[8,64,1536]{2,1,0:T(8,128)(2,1)} reshape(bf16[8,64,24,64]{3,2,1,0:T(8,128)(2,1)S(1)} %convert_bitcast_fusion) | data formatting | bytes 3145728 | tf_op jit(solution)/shard_map/reshape | solution.py:26
  32.3 1.6 constant_dynamic-update-slice_fusion.2
  36.7 1.5 collective-permute-start.5
  38.9 2.2 collective-permute-done.5
  41.6 1.5 gather_fusion
  43.3 1.8 fusion.1
  45.1 3.4 %reshape.105 = bf16[4,64,1536]{2,1,0:T(8,128)(2,1)} reshape(bf16[4,64,24,64]{3,2,1,0:T(8,128)(2,1)} %fusion.1) | data formatting | bytes 1572864 | tf_op jit(solution)/shard_map/reshape | solution.py:26
  48.5 1.5 gather_fusion.2
  50.2 1.8 fusion.2
  52.0 3.4 %reshape.107 = bf16[4,64,1536]{2,1,0:T(8,128)(2,1)} reshape(bf16[4,64,24,64]{3,2,1,0:T(8,128)(2,1)} %fusion.2) | data formatting | bytes 1572864 | tf_op jit(solution)/shard_map/reshape | solution.py:26
  55.4 1.3 constant_dynamic-update-slice_fusion.1
  56.9 1.8 gather_fusion.4
  58.7 2.0 gather_fusion.5
  60.6 1.9 gather_fusion.6
  62.6 1.9 gather_fusion.7
  64.5 1.9 gather_fusion.8
  66.4 1.9 gather_fusion.9
  68.4 2.0 gather_fusion.10
  70.4 2.2 fusion.4
  74.7 0.8 copy-done.2
  77.5 0.8 copy-done
  79.0 4.8 %convolution_bitcast_fusion = f32[512,1536]{1,0:T(8,128)} fusion(bf16[8,64,512]{2,1,0:T(8,128)(2,1)} %reshape.102, f32[8,64,1536]{2,1,0:T(8,128)S(1)} %convolution_add_fusion.1, bf16[8,64,1536]{2,1,0:T(8,128)(2,1)} %gather_fusion.10, bf16[8,64,448]{2,1,0:T(8,128)(2,1)} %bitcast.75, bf16[8]{0:T(256)(128)(2,1)S(1)} %copy-done.16), kind=kOutput, calls=%fused_computation.17 | convolution fusion | flops 907575296 | bytes 8519696 | tf_op jit(solution)/shard_map/nbc,nbw->cw/dot_general | solution.py:68
  83.8 138.3 %all-reduce.2.cloned.1.call-done = f32[512,1536]{1,0:T(8,128)} async-done(((f32[512,1536]{1,0:T(8,128)}), f32[512,1536]{1,0:T(8,128)}) %all-reduce.2.cloned.1.call-update) | async-done | bytes 3145744 | tf_op jit(solution)/shard_map/psum | solution.py:67
  222.2 1.6 dynamic-slice_bitcast_fusion
  (65 shorter events, 11.4 us)
Async XLA Ops:
  6.5 215.6 %all-reduce.2.cloned.1.call-start = ((), (), s32[]{:S(2)}) async-start(), calls=%async_computation | async-start | bytes 6291456 | tf_op jit(solution)/shard_map/psum | solution.py:67
  6.5 35.1 %collective-permute-start = (bf16[8,64,256]{2,1,0:T(8,128)(2,1)}, bf16[8,64,256]{2,1,0:T(8,128)(2,1)}, u32[]{:S(2)}, u32[]{:S(2)}) collective-permute-start(bf16[8,64,256]{2,1,0:T(8,128)(2,1)} %bitcast.81), channel_id=1, source_target_pairs={{0,16},{16,32},{32,48},{48,64},{64,80},{80,96},{96,112},{112,128},... | collective-permute-start | bytes 786440 | tf_op jit(solution)/shard_map/ppermute | solution.py:14
  11.2 37.4 %collective-permute-start.3 = (bf16[8,64,256]{2,1,0:T(8,128)(2,1)}, bf16[8,64,256]{2,1,0:T(8,128)(2,1)}, u32[]{:S(2)}, u32[]{:S(2)}) collective-permute-start(bf16[8,64,256]{2,1,0:T(8,128)(2,1)} %bitcast.82), channel_id=1, source_target_pairs={{16,0},{32,16},{48,32},{64,48},{80,64},{96,80},{112,96},{128,112},... | collective-permute-start | bytes 786440 | tf_op jit(solution)/shard_map/ppermute | solution.py:14
  12.5 24.2 %collective-permute-start.1 = (s32[8]{0:T(128)}, s32[8]{0:T(128)S(1)}, u32[]{:S(2)}, u32[]{:S(2)}) collective-permute-start(s32[8]{0:T(128)} %bitcast.85), channel_id=1, source_target_pairs={{0,16},{16,32},{32,48},{48,64},{64,80},{80,96},{96,112},{112,128},... | collective-permute-start | bytes 104 | tf_op jit(solution)/shard_map/ppermute | solution.py:14
  16.5 21.8 %collective-permute-start.4 = (s32[8]{0:T(128)}, s32[8]{0:T(128)S(1)}, u32[]{:S(2)}, u32[]{:S(2)}) collective-permute-start(s32[8]{0:T(128)} %bitcast.86), channel_id=1, source_target_pairs={{16,0},{32,16},{48,32},{64,48},{80,64},{96,80},{112,96},{128,112},... | collective-permute-start | bytes 104 | tf_op jit(solution)/shard_map/ppermute | solution.py:14
  18.5 19.8 %collective-permute-start.2 = (s32[8,4]{1,0:T(8,128)S(1)}, s32[8,4]{1,0:T(8,128)S(1)}, u32[]{:S(2)}, u32[]{:S(2)}) collective-permute-start(s32[8,4]{1,0:T(8,128)S(1)} %copy.12), channel_id=1, source_target_pairs={{0,16},{16,32},{32,48},{48,64},{64,80},{80,96},{96,112},{112,128},... | collective-permute-start | bytes 392 | tf_op jit(solution)/shard_map/ppermute | solution.py:14
  23.7 2.8 %copy-start.5 = (bf16[8,64,4,64]{3,2,1,0:T(4,128)(2,1)}, bf16[8,64,4,64]{3,2,1,0:T(4,128)(2,1)S(1)}, u32[]{:S(2)}) copy-start(bf16[8,64,4,64]{3,2,1,0:T(4,128)(2,1)S(1)} %reshape_squeeze.4) | copy-start | bytes 786436
  32.3 1.6 copy-start.8
  32.3 2.0 copy-start.15
  36.7 4.3 %collective-permute-start.5 = (s32[8,4]{1,0:T(8,128)S(1)}, s32[8,4]{1,0:T(8,128)S(1)}, u32[]{:S(2)}, u32[]{:S(2)}) collective-permute-start(s32[8,4]{1,0:T(8,128)S(1)} %copy.12), channel_id=1, source_target_pairs={{16,0},{32,16},{48,32},{64,48},{80,64},{96,80},{112,96},{128,112},... | collective-permute-start | bytes 392 | tf_op jit(solution)/shard_map/ppermute | solution.py:14
  55.4 1.4 copy-start.6
  68.4 2.1 copy-start.14
  70.4 2.2 copy-start.4
  70.4 2.3 copy-start.7
  70.4 2.3 copy-start.13
  72.7 1.4 copy-start.3
  72.7 1.4 copy-start.12
  74.1 1.4 copy-start.2
  74.1 1.4 copy-start.11
  75.5 1.4 copy-start.1
  75.5 1.4 copy-start.10
  76.9 1.4 copy-start
  76.9 1.4 copy-start.9
  78.3 0.7 copy-start.16
Sparse Core Ops, SparseCore 0:
  83.9 138.1 all-reduce.1
where the time goes:
time: 231 us
  waiting for transfers between devices  141 us (61%)
  local copies, waits for them, and re-layouts  39.2 us (17%)
  matrix products  17.1 us (7%)
  starting transfers between devices  16.6 us (7%)
  between operations  13.7 us (6%)
  other arithmetic  3.52 us (2%)
    psum x1, waiting for transfers between devices, body(): lax.psum(jnp.einsum('nbc,nbw->cw', own, product, preferred_element_type=j...  138 us
    ppermute x6, starting transfers between devices, shifted(): return lax.ppermute(value, axis, pairs)  16.6 us
    gather x7, local copies, waits for them, and re-layouts, body(): picked = extended[acol[:, slot]]  13.5 us
    reshape x4, local copies, waits for them, and re-layouts, dense_rows(): return dense.astype(jnp.bfloat16).reshape(count, size, width_blocks * size)  11.2 us
    dot_general x4, matrix products, dense_rows(): jnp.einsum('rkc,rbka->rbca', onehot, parts, preferred_element_type=jnp.fl...  7.01 us
    unnamed x37, local copies, waits for them, and re-layouts  6.28 us
    dot_general x6, matrix products, body(): jnp.einsum('nij,njw->niw', ablock, picked, preferred_element_type=jnp.flo...  5.28 us
    dot_general x1, matrix products, body(): jnp.einsum('nbc,nbw->cw', own, product, preferred_element_type=jnp.float32)  4.77 us
  transfers between devices with their start and end apart: 7, of which 2 were waited for; matrix products, arithmetic and copies ran while one was open for 10% of the time, Pallas kernels for 0%

commit v1 on v0

v1 whole, which is shorter than its diff:
```python
import jax
import jax.numpy as jnp
from jax import lax
from jax.experimental import pallas as pl
from jax.experimental.pallas import tpu as pltpu
from jax.sharding import PartitionSpec as P

KA = 7
KS = 3
KP = 4
NCOL = 8
G = 4
NB = 8
BS = 64
W = NCOL * BS
MESH = pl.DeviceIdType.MESH
LEFT, OWN, RIGHT = 0, 1, 2
GHOST = G * BS


def doubled(tile, low):
    turned = pltpu.roll(tile, BS, 1)
    return jnp.where(low, tile, turned), jnp.where(low, turned, tile)


def kernel(nx, ny, acol, mush, pcol, sends, a_hbm, p_hbm, out_ref,
           a_v, p_v, gsend, grecv, ext, gext, amat, own_t, keep, psend, precv,
           csa, csb, cra, crb,
           load_sem, gs_sem, gr_sem, ps_sem, pr_sem, sa_sem, ra_sem, sb_sem, rb_sem):
    gx = lax.axis_index("gx")
    gy = lax.axis_index("gy")
    yc = gy // 2
    core = gy % 2
    sign = 1 - 2 * core
    west = (gx + nx - 1) % nx
    east = (gx + 1) % nx
    chips = ny // 2

    def chip(by):
        return (yc + sign * by + chips) % chips

    sibling = (gx, yc * 2 + 1 - core)
    ahead = (gx, chip(1) * 2 + core)
    behind = (gx, chip(-1) * 2 + core)

    barrier = pltpu.get_barrier_semaphore()
    for device in ((west, gy), (east, gy), sibling, ahead, behind):
        pl.semaphore_signal(barrier, inc=1, device_id=device, device_id_type=MESH)

    load_p = pltpu.make_async_copy(p_hbm.at[0], p_v, load_sem.at[0])
    load_a = pltpu.make_async_copy(a_hbm.at[0], a_v, load_sem.at[1])
    load_p.start()
    load_a.start()

    def remote(src, dst, send, recv, device):
        return pltpu.make_async_remote_copy(
            src_ref=src, dst_ref=dst, send_sem=send, recv_sem=recv,
            device_id=device, device_id_type=MESH)

    ghosts = [
        remote(gsend.at[side], grecv.at[side], gs_sem.at[side], gr_sem.at[side],
               ((east, west)[side], gy))
        for side in range(2)
    ]
    pairs = [remote(psend.at[part], precv.at[part], ps_sem.at[part], pr_sem.at[part], sibling)
             for part in range(3)]
    chain_a = [[remote(csa.at[part, s], cra.at[part, s], sa_sem.at[part, s], ra_sem.at[part, s], ahead)
                for s in range(4)] for part in range(3)]
    chain_b = [[remote(csb.at[part, s], crb.at[part, s], sb_sem.at[part, s], rb_sem.at[part, s], behind)
                for s in range(3)] for part in range(3)]

    low = lax.broadcasted_iota(jnp.int32, (BS, 2 * BS), 1) < BS
    half = lax.broadcasted_iota(jnp.int32, (1, 2 * BS), 1) // BS
    half_f = half.astype(jnp.float32)

    load_p.wait()
    row_of = lax.broadcasted_iota(jnp.int32, (16, 256), 0)
    for side in range(2):
        codes = jnp.zeros((16, 256), jnp.int32)
        for i in range(G):
            row = sends[0, (1 - side) * G + i]
            gsend[side, i * BS:(i + 1) * BS, :] = p_v[row]
            for j in range(KP):
                codes = jnp.where(row_of == i * KP + j, pcol[0, row, j], codes)
        gsend[side, GHOST:GHOST + 16, :] = codes.astype(jnp.float32).astype(jnp.bfloat16)
    pl.semaphore_wait(barrier, 5)
    for side in range(2):
        ghosts[side].start()

    def placed(block, hits):
        parts = doubled(block[:, :128], low) + doubled(block[:, 128:], low)
        tiles = []
        for q in range(NCOL // 2):
            total = parts[0] * hits(0, q)
            for j in range(1, KP):
                total = total + parts[j] * hits(j, q)
            tiles.append(total.astype(jnp.bfloat16))
        return tiles

    @pl.loop(0, NB)
    def _(n):
        def hits(j, q):
            return jnp.where(half + 2 * q == pcol[0, n, j], 1.0, 0.0)

        for q, tile in enumerate(placed(p_v[n].astype(jnp.float32), hits)):
            ext[n, :, q * 128:(q + 1) * 128] = tile

    own_t[...] = ext[...].reshape(NB * BS, W).T.reshape(NCOL, 2, BS // 2, NB * BS)

    def spread(n, first, tiles):
        block = a_v[n].astype(jnp.float32)
        parts = []
        for m in range(3):
            parts += doubled(block[:, m * 128:(m + 1) * 128], low)
        last = block[:, 384:448]
        parts.append(jnp.concatenate([last, last], axis=1))
        codes = []
        for k in range(KA):
            code = acol[0, n, k]
            codes.append(code if k < KS else jnp.where(mush[0, n] > 0, code, -1))
        for q in range(first, first + tiles):
            total = parts[0] * jnp.where(half + 2 * q == codes[0], 1.0, 0.0)
            for k in range(1, KA):
                total = total + parts[k] * jnp.where(half + 2 * q == codes[k], 1.0, 0.0)
            high = total.astype(jnp.bfloat16)
            rest = (total - high.astype(jnp.float32)).astype(jnp.bfloat16)
            amat[0, n, :, q * 128:(q + 1) * 128] = high
            amat[1, n, :, q * 128:(q + 1) * 128] = rest

    def product(lo, hi, rows):
        wide = hi - lo
        high = amat[0, :, :, lo:hi].reshape(NB * BS, wide)
        rest = amat[1, :, :, lo:hi].reshape(NB * BS, wide)
        total = jnp.dot(high, rows, preferred_element_type=jnp.float32)
        total = total + jnp.dot(rest, rows, preferred_element_type=jnp.float32)
        return total.astype(jnp.bfloat16)

    def tile_rows(part, ap):
        mine = own_t[:, pl.ds(1 - core, 1)].reshape(NCOL * BS // 2, NB * BS)
        away = jnp.dot(mine, ap, preferred_element_type=jnp.float32)
        psend[part] = away.astype(jnp.bfloat16).reshape(NCOL, BS // 2, W)
        pairs[part].start()
        mine = own_t[:, pl.ds(core, 1)].reshape(NCOL * BS // 2, NB * BS)
        stay = jnp.dot(mine, ap, preferred_element_type=jnp.float32)
        keep[part] = stay.reshape(NCOL, BS // 2, W)

    def summed(part, t):
        return keep[part, t] + precv[part, t].astype(jnp.float32)

    def hop(part, s):
        value = summed(part, chip(4 - s))
        if s > 0:
            chain_a[part][s - 1].wait_recv()
            value = value + cra[part, s - 1].astype(jnp.float32)
        csa[part, s] = value.astype(jnp.bfloat16)
        chain_a[part][s].start()
        if s < 3:
            value = summed(part, chip(s - 3))
            if s > 0:
                chain_b[part][s - 1].wait_recv()
                value = value + crb[part, s - 1].astype(jnp.float32)
            csb[part, s] = value.astype(jnp.bfloat16)
            chain_b[part][s].start()

    def finish(part):
        value = summed(part, yc)
        chain_b[part][2].wait_recv()
        value = value + crb[part, 2].astype(jnp.float32)
        chain_a[part][3].wait_recv()
        value = value + cra[part, 3].astype(jnp.float32)
        out_ref[0, :, part * W:(part + 1) * W] = value

    load_a.wait()

    @pl.loop(0, NB)
    def _(n):
        spread(n, 0, 4)

    tile_rows(OWN, product(0, W, ext[...].reshape(NB * BS, W)))

    @pl.loop(0, NB)
    def _(n):
        spread(n, 4, 4)

    def ghost_product(side):
        ghosts[side].wait_recv()
        there = (gx > 0, gx < nx - 1)[side]
        codes = jnp.where(there, grecv[side, GHOST:GHOST + 16, :128].astype(jnp.float32), -1.0)
        for i in range(G):
            def hits(j, q):
                code = codes[i * KP + j:i * KP + j + 1, :]
                return jnp.where(half_f + 2.0 * q == code, 1.0, 0.0)

            block = grecv[side, i * BS:(i + 1) * BS, :].astype(jnp.float32)
            for q, tile in enumerate(placed(block, hits)):
                gext[side, i * BS:(i + 1) * BS, q * 128:(q + 1) * 128] = tile
        lo = W + side * GHOST
        return product(lo, lo + GHOST, gext[side])

    ap = ghost_product(0)
    pairs[OWN].wait_recv()
    hop(OWN, 0)
    tile_rows(LEFT, ap)
    ap = ghost_product(1)
    hop(OWN, 1)
    tile_rows(RIGHT, ap)
    pairs[LEFT].wait_recv()
    hop(LEFT, 0)
    hop(OWN, 2)
    pairs[RIGHT].wait_recv()
    hop(RIGHT, 0)
    hop(LEFT, 1)
    hop(OWN, 3)
    hop(RIGHT, 1)
    hop(LEFT, 2)
    finish(OWN)
    hop(RIGHT, 2)
    hop(LEFT, 3)
    hop(RIGHT, 3)
    finish(LEFT)
    finish(RIGHT)
    for copy in ghosts + pairs + sum(chain_a, []) + sum(chain_b, []):
        copy.wait_send()


def solution(mesh):
    nx, ny = mesh.shape["gx"], mesh.shape["gy"]

    def body(a_blocks, a_cols, mushy, p_blocks, p_cols, send_rows):
        smem = pl.BlockSpec(memory_space=pltpu.SMEM)
        hbm = pl.BlockSpec(memory_space=pl.ANY)
        bf16, f32 = jnp.bfloat16, jnp.float32
        dma = pltpu.SemaphoreType.DMA
        rows = BS // 2

        def run(*refs):
            kernel(nx, ny, *refs)

        return pl.pallas_call(
            run,
            name="galerkin",
            out_shape=jax.ShapeDtypeStruct((1, rows, 3 * W), f32),
            in_specs=[smem, smem, smem, smem, hbm, hbm],
            out_specs=pl.BlockSpec(memory_space=pltpu.VMEM),
            scratch_shapes=[
                pltpu.VMEM((NB, BS, KA * BS), bf16),
                pltpu.VMEM((NB, BS, KP * BS), bf16),
                pltpu.VMEM((2, GHOST + 16, KP * BS), bf16),
                pltpu.VMEM((2, GHOST + 16, KP * BS), bf16),
                pltpu.VMEM((NB, BS, W), bf16),
                pltpu.VMEM((2, GHOST, W), bf16),
                pltpu.VMEM((2, NB, BS, 2 * NB * BS), bf16),
                pltpu.VMEM((NCOL, 2, rows, NB * BS), bf16),
                pltpu.VMEM((3, NCOL, rows, W), f32),
                pltpu.VMEM((3, NCOL, rows, W), bf16),
                pltpu.VMEM((3, NCOL, rows, W), bf16),
                pltpu.VMEM((3, 4, rows, W), bf16),
                pltpu.VMEM((3, 3, rows, W), bf16),
                pltpu.VMEM((3, 4, rows, W), bf16),
                pltpu.VMEM((3, 3, rows, W), bf16),
                dma((2,)), dma((2,)), dma((2,)), dma((3,)), dma((3,)),
                dma((3, 4)), dma((3, 4)), dma((3, 3)), dma((3, 3)),
            ],
            compiler_params=pltpu.CompilerParams(
                collective_id=0, has_side_effects=True, vmem_limit_bytes=48 * 1024 * 1024),
        )(a_cols, mushy, p_cols, send_rows, a_blocks, p_blocks)

    placed_as = (
        P("gx", "gy", None, None),
        P("gx", "gy", None),
        P("gx", "gy"),
        P("gx", "gy", None, None),
        P("gx", "gy", None),
        P("gx", "gy"),
    )
    return jax.shard_map(
        body, mesh=mesh, in_specs=placed_as, out_specs=P("gx", "gy", None), check_vma=False
    )
```

time: 231 us -> 44.9 us (0.19)
  the two profiles are of different devices: /device:TPU:1 before, /device:TPU:8 now
where the time goes in v1:
time: 44.9 us; the launch traced here: 44.7 us
  Pallas kernels  40.5 us (90%)
  local copies, waits for them, and re-layouts  4.12 us (9%)
    pallas_call x1, Pallas kernels, body(): pl.pallas_call(run, name='galerkin', out_shape=jax.ShapeDtypeStruct((1, r...  40.5 us
    unnamed x13, local copies, waits for them, and re-layouts  4.12 us

profile of v1, /device:TPU:8, one launch (start us, length us, event | category | flops | bytes accessed | tf_op | source)
XLA Modules:
  0.0 44.7 jit_solution(11236829016770308590)
XLA Ops:
  0.0 0.0 copy-start.4
  0.0 0.8 %copy.7.refs_0_ = s32[1,8,7]{2,1,0:T(8,128)S(1)} copy(s32[1,8,7]{1,0,2:T(1,128)} %param.7) | data formatting | bytes 448 | tf_op args[1]
  0.8 0.0 copy-done.4
  0.8 0.0 copy-start.2
  0.8 0.0 copy-start.3
  0.8 0.1 copy.8.refs_2_
  0.9 0.6 %copy-done.2 = s32[1,8]{1,0:T(1,128)S(1)} copy-done((s32[1,8]{1,0:T(1,128)S(1)}, s32[1,8]{1,0:T(1,128)}, u32[]{:S(2)}) %copy-start.2) | copy-done | bytes 56
  1.4 0.0 copy-done.3
  1.5 0.0 copy-start
  1.5 1.0 %copy-done = bf16[1,8,64,448]{3,2,1,0:T(8,128)(2,1)S(1)} copy-done((bf16[1,8,64,448]{3,2,1,0:T(8,128)(2,1)S(1)}, bf16[1,8,64,448]{3,2,1,0:T(8,128)(2,1)}, u32[]{:S(2)}) %copy-start) | copy-done | bytes 458776
  2.5 0.0 copy-start.1
  2.5 0.9 %copy-done.1 = bf16[1,8,64,256]{3,2,1,0:T(8,128)(2,1)S(1)} copy-done((bf16[1,8,64,256]{3,2,1,0:T(8,128)(2,1)S(1)}, bf16[1,8,64,256]{3,2,1,0:T(8,128)(2,1)}, u32[]{:S(2)}) %copy-start.1) | copy-done | bytes 262168
  3.4 40.5 %galerkin.1 = f32[1,32,1536]{2,1,0:T(8,128)S(1)} custom-call(s32[1,8,7]{2,1,0:T(8,128)S(1)} %copy.7.refs_0_, s32[1,8]{1,0:T(1,128)S(1)} %copy-done.2, s32[1,8,4]{2,1,0:T(8,128)S(1)} %copy.8.refs_2_, s32[1,8]{1,0:T(1,128)S(1)} %copy-done.3, bf16[1,8,64,448]{3,2,1,0:T(8,128)(2,1)S(1)} %copy-done, bf16[1,8,64,256]{3,2,1,0:T(8,128)(2,1)S(1)} %copy-done.1), custom_call_target="tpu_custom_call" | custom-call | tf_op jit(solution)/shard_map/galerkin/pallas_call | solution.py:239
  44.0 0.7 %copy.10 = f32[1,32,1536]{2,1,0:T(8,128)} copy(f32[1,32,1536]{2,1,0:T(8,128)S(1)} %galerkin.1) | data formatting | bytes 393216
Async XLA Ops:
  0.0 0.8 %copy-start.4 = (s32[1,8,4]{1,2,0:T(4,128)S(1)}, s32[1,8,4]{1,2,0:T(4,128)}, u32[]{:S(2)}) copy-start(s32[1,8,4]{1,2,0:T(4,128)} %param.10) | copy-start | bytes 388
  0.8 0.7 %copy-start.2 = (s32[1,8]{1,0:T(1,128)S(1)}, s32[1,8]{1,0:T(1,128)}, u32[]{:S(2)}) copy-start(s32[1,8]{1,0:T(1,128)} %refs_1_.1) | copy-start | bytes 100
  0.8 0.7 %copy-start.3 = (s32[1,8]{1,0:T(1,128)S(1)}, s32[1,8]{1,0:T(1,128)}, u32[]{:S(2)}) copy-start(s32[1,8]{1,0:T(1,128)} %refs_3_.1) | copy-start | bytes 100
  1.5 1.0 %copy-start = (bf16[1,8,64,448]{3,2,1,0:T(8,128)(2,1)S(1)}, bf16[1,8,64,448]{3,2,1,0:T(8,128)(2,1)}, u32[]{:S(2)}) copy-start(bf16[1,8,64,448]{3,2,1,0:T(8,128)(2,1)} %refs_4_.1) | copy-start | bytes 1376260
  2.5 0.9 %copy-start.1 = (bf16[1,8,64,256]{3,2,1,0:T(8,128)(2,1)S(1)}, bf16[1,8,64,256]{3,2,1,0:T(8,128)(2,1)}, u32[]{:S(2)}) copy-start(bf16[1,8,64,256]{3,2,1,0:T(8,128)(2,1)} %refs_5_.1) | copy-start | bytes 786436
